TPU v7x, 256 devices: a whole 4x4x8 slice. The times are simulated.
256 devices in a mesh: kv: 4 (over y), blk: 64 (over z, x, core).
Axes of the slice: x: 4, y: 4, z: 8, core: 2. Of those that a mesh axis runs over, the one named last changes fastest.
Arguments:
- embeds: bfloat16 [3, 512, 4096], P(None, None, 'blk'), may hold values from -6 to 6
- attn_gain: float32 [4096], P('blk'), may hold values from 0.25 to 1.75
- w_query: bfloat16 [4096, 4096], P('blk', 'kv'), may hold values from -0.1875 to 0.1875
- w_key: bfloat16 [4096, 512], P('blk', 'kv'), may hold values from -0.09375 to 0.09375
- w_value: bfloat16 [4096, 512], P('blk', 'kv'), may hold values from -0.09375 to 0.09375
- w_out: bfloat16 [4096, 4096], P('kv', 'blk'), may hold values from -0.375 to 0.375
- cache_kv: bfloat16 [2048, 4, 2, 128, 128], P('blk', 'kv'), may hold values from -102 to 102, as said below
- lengths: int32 [512], replicated, may hold values from 1 to 8192, as said below
- block_table: int32 [512, 64], replicated, may hold values from 0 to 2048, as said below
- parents: int32 [3, 512], replicated, may hold values from 0 to 511, as said below
Outputs:
- out_rows: bfloat16 [3, 512, 4096], P(None, None, 'blk')
- appended: bfloat16 [3, 512, 4, 2, 128], P(None, 'blk', 'kv')
Inputs may be any that keep to these rules, and one draw needn't show every extreme that they name: `lengths`: one beam holds exactly 8192 tokens. `block_table`: row b names the slots of beam b's blocks of 128 tokens in order; entries at and past ceil(lengths[b] / 128) equal 2048; no slot is named twice. parents[s, b] lies in the aligned group of 8 beams that holds b. `cache_kv`: slots that no row of block_table names are never read.
All inputs are finite; a program needn't handle non-finite values.
Results may differ from a plain program's by a relative error of at most 0.0044.
The roundings to bfloat16 on the way count: a program that leaves them out, or rounds other values in their place, can miss the bound.
Values may be sent and summed in bfloat16 or wider, within the bound.
No kernel may reach another device: no remote copies, remote signals or barrier semaphores. Data moves between devices by JAX's collectives and lax.ppermute only.
A program may use at most 64 MiB of HBM per device.

v0:
```python
import math
import jax
import jax.numpy as jnp
from jax import lax
from jax.sharding import PartitionSpec as P

GROUP = 8
NEGATIVE = -1e30
EPSILON = 1e-05
ROPE_BASE = 5000000.0


def rotate(vector, position):
    half_dim = vector.shape[-1] // 2
    exponent = jnp.arange(half_dim, dtype=jnp.float32) * (2.0 / vector.shape[-1])
    frequency = ROPE_BASE ** (-exponent)
    angles = position.astype(jnp.float32)[:, None] * frequency[None, :]
    target_shape = (position.shape[0],) + (1,) * (vector.ndim - 2) + (half_dim,)
    cosines = jnp.cos(angles).reshape(target_shape)
    sine_part = jnp.sin(angles).reshape(target_shape)
    first_half = vector[..., :half_dim]
    second_half = vector[..., half_dim:]
    return jnp.concatenate(
        [
            first_half * cosines - second_half * sine_part,
            second_half * cosines + first_half * sine_part,
        ],
        axis=-1,
    )


def body(
    embeds, attn_gain, w_query, w_key, w_value, w_out, cache_kv, lengths, block_table, parents
):
    axis_count = lax.axis_size("blk")
    shard_index = lax.axis_index("blk")
    step_total, beam_count, width_part = embeds.shape
    beams_here = beam_count // axis_count
    slot_count = cache_kv.shape[0]
    total_slots = slot_count * axis_count
    block_len = cache_kv.shape[3]
    head_dim = cache_kv.shape[4]
    heads_per_group = w_query.shape[1] // head_dim
    group_count = beam_count // GROUP
    model_width = width_part * axis_count
    scaling = 1.0 / math.sqrt(head_dim)
    row_offset = shard_index * beams_here
    joined_weights = jnp.concatenate([w_query, w_key, w_value], axis=1)
    cached_keys = cache_kv[:, 0, 0]
    cached_values = cache_kv[:, 0, 1]
    max_blocks = block_table.shape[1]
    beam_ids = jnp.broadcast_to(jnp.arange(beam_count, dtype=jnp.int32)[:, None], block_table.shape)
    block_ids = jnp.broadcast_to(
        jnp.arange(max_blocks, dtype=jnp.int32)[None, :], block_table.shape
    )
    flat_table = block_table.reshape(-1)
    owner_all = jnp.full((total_slots + 1,), -1, jnp.int32).at[flat_table].set(beam_ids.reshape(-1))
    logical_all = jnp.zeros((total_slots + 1,), jnp.int32).at[flat_table].set(block_ids.reshape(-1))
    owner_beam = lax.dynamic_slice_in_dim(owner_all, shard_index * slot_count, slot_count)
    logical_block = lax.dynamic_slice_in_dim(logical_all, shard_index * slot_count, slot_count)
    filled = owner_beam >= 0
    safe_owner = jnp.maximum(owner_beam, 0)
    group_of = safe_owner // GROUP
    group_onehot = (
        (group_of[:, None] == jnp.arange(group_count, dtype=jnp.int32)[None, :]) & filled[:, None]
    ).astype(jnp.float32)
    token_index = jnp.arange(block_len, dtype=jnp.int32)
    in_length = (
        logical_block[:, None] * block_len + token_index[None, :] < lengths[safe_owner][:, None]
    )
    members = group_of[:, None] * GROUP + jnp.arange(GROUP, dtype=jnp.int32)[None, :]
    root_beams = jnp.arange(beam_count, dtype=jnp.int32)
    new_keys = jnp.zeros((step_total, beams_here, head_dim), jnp.bfloat16)
    new_values = jnp.zeros((step_total, beams_here, head_dim), jnp.bfloat16)
    outputs = []
    for step_index in range(step_total):
        root_beams = root_beams[parents[step_index]]
        local_parent = (
            lax.dynamic_slice_in_dim(parents[step_index], row_offset, beams_here) - row_offset
        )
        new_keys = new_keys[:, local_parent]
        new_values = new_values[:, local_parent]
        stream = embeds[step_index].astype(jnp.float32)
        squares = lax.psum(jnp.sum(stream * stream, axis=1), "blk")
        inverse_rms = lax.rsqrt(squares / model_width + EPSILON)
        normed = (stream * inverse_rms[:, None] * attn_gain[None, :]).astype(jnp.bfloat16)
        projected = lax.psum_scatter(
            jnp.dot(normed, joined_weights, preferred_element_type=jnp.float32),
            "blk",
            scatter_dimension=0,
            tiled=True,
        )
        position = (
            lax.dynamic_slice_in_dim(lengths[root_beams], row_offset, beams_here) + step_index
        )
        rotated_query = rotate(
            projected[:, : heads_per_group * head_dim].reshape(
                beams_here, heads_per_group, head_dim
            ),
            position,
        ).astype(jnp.bfloat16)
        key_new = rotate(
            projected[:, heads_per_group * head_dim : (heads_per_group + 1) * head_dim], position
        ).astype(jnp.bfloat16)
        value_new = projected[:, (heads_per_group + 1) * head_dim :].astype(jnp.bfloat16)
        new_keys = new_keys.at[step_index].set(key_new)
        new_values = new_values.at[step_index].set(value_new)
        queries = lax.all_gather(
            rotated_query.reshape(beams_here, heads_per_group * head_dim), "blk", axis=0, tiled=True
        )
        slot_query = queries.reshape(group_count, GROUP * heads_per_group, head_dim)[group_of]
        scores = (
            jnp.einsum("sqd,skd->sqk", slot_query, cached_keys, preferred_element_type=jnp.float32)
            * scaling
        )
        scores = scores.reshape(slot_count, GROUP, heads_per_group, block_len)
        active = ((root_beams[members] == owner_beam[:, None])[:, :, None] & in_length[:, None, :])[
            :, :, None, :
        ]
        slot_top = jnp.max(jnp.where(active, scores, NEGATIVE), axis=-1)
        group_top = jnp.max(
            jnp.where(group_onehot[:, :, None, None] > 0, slot_top[:, None], NEGATIVE), axis=0
        ).reshape(beam_count, heads_per_group)
        latest_key_rows = new_keys[: step_index + 1]
        new_scores = (
            jnp.einsum(
                "pam,fpm->paf", rotated_query, latest_key_rows, preferred_element_type=jnp.float32
            )
            * scaling
        )
        own_top = jnp.maximum(
            lax.dynamic_slice_in_dim(group_top, row_offset, beams_here),
            jnp.max(new_scores, axis=-1),
        )
        local_top = lax.dynamic_update_slice_in_dim(group_top, own_top, row_offset, 0)
        ceiling = lax.pmax(local_top, "blk")
        slot_ceiling = ceiling.reshape(group_count, GROUP, heads_per_group)[group_of]
        prob_weights = jnp.exp(jnp.where(active, scores - slot_ceiling[..., None], NEGATIVE))
        slot_denominator = jnp.sum(prob_weights, axis=-1)
        slot_numer = jnp.einsum(
            "sgqk,skd->sgqd",
            prob_weights.astype(jnp.bfloat16),
            cached_values,
            preferred_element_type=jnp.float32,
        )
        numerator = jnp.einsum(
            "sg,sx->gx",
            group_onehot,
            slot_numer.reshape(slot_count, -1),
            precision=lax.Precision.HIGHEST,
        ).reshape(beam_count, heads_per_group, head_dim)
        denominator = jnp.einsum(
            "sg,sx->gx",
            group_onehot,
            slot_denominator.reshape(slot_count, -1),
            precision=lax.Precision.HIGHEST,
        ).reshape(beam_count, heads_per_group)
        own_ceiling = lax.dynamic_slice_in_dim(ceiling, row_offset, beams_here)
        new_weights = jnp.exp(new_scores - own_ceiling[..., None])
        updated_denominator = jnp.sum(new_weights, axis=-1)
        new_numer = jnp.einsum(
            "pjz,zpc->pjc",
            new_weights.astype(jnp.bfloat16),
            new_values[: step_index + 1],
            preferred_element_type=jnp.float32,
        )
        numerator, denominator = (
            lax.psum_scatter(numerator, "blk", scatter_dimension=0, tiled=True),
            lax.psum_scatter(denominator, "blk", scatter_dimension=0, tiled=True),
        )
        own_rows = (
            ((numerator + new_numer) / (denominator + updated_denominator)[..., None])
            .astype(jnp.bfloat16)
            .reshape(beams_here, heads_per_group * head_dim)
        )
        attended = lax.all_gather(own_rows, "blk", axis=0, tiled=True)
        partial_value = jnp.dot(attended, w_out, preferred_element_type=jnp.float32)
        head_total = lax.psum(partial_value, "kv")
        outputs.append((stream + head_total).astype(jnp.bfloat16))
    appended = jnp.stack([new_keys, new_values], axis=2)[:, :, None]
    return (jnp.stack(outputs), appended)


def solution(mesh):
    return jax.shard_map(
        body,
        mesh=mesh,
        in_specs=(
            P(None, None, "blk"),
            P("blk"),
            P("blk", "kv"),
            P("blk", "kv"),
            P("blk", "kv"),
            P("kv", "blk"),
            P("blk", "kv", None, None, None),
            P(),
            P(),
            P(),
        ),
        out_specs=(P(None, None, "blk"), P(None, "blk", "kv", None, None)),
        check_vma=False,
    )
```

profile of v0, /device:TPU:2, one launch (start us, length us, event | category | flops | bytes accessed | tf_op | source)
XLA Modules:
  0.0 1692.4 jit_solution(13006681837210420839)
XLA Ops:
  9.2 128.5 %all-reduce.7 = (f32[512]{0:T(512)S(1)}, f32[512]{0:T(512)S(1)}, f32[512]{0:T(512)S(1)}) all-reduce(f32[512]{0:T(512)S(1)} %get-tuple-element.102, f32[512]{0:T(512)S(1)} %get-tuple-element.101, f32[512]{0:T(512)S(1)} %get-tuple-element.100), channel_id=1, replica_groups=mesh['kv'=4,'blk'=64] {'blk'}, use_global_device_ids=true, to_apply=%region_25.26 | all-reduce | flops 1536 | bytes 12288 | tf_op jit(solution)/shard_map/psum | solution.py:84
  139.2 3.0 fusion.73
  142.2 2.1 fusion.76
  144.3 2.2 fusion.79
  147.2 3.5 gather_fusion
  150.7 3.5 gather_fusion.6
  154.4 3.5 gather_fusion.3
  157.9 3.5 gather_fusion.14
  161.4 3.5 gather_fusion.16
  164.9 3.5 gather_fusion.8
  170.3 179.9 %all-reduce.14.cloned.1.call-done = (f32[512,1280]{1,0:T(8,128)}, f32[512,1280]{1,0:T(8,128)}, f32[512,1280]{1,0:T(8,128)}) async-done(((f32[512,1280]{1,0:T(8,128)}, f32[512,1280]{1,0:T(8,128)}, f32[512,1280]{1,0:T(8,128)}), (f32[512,1280]{1,0:T(8,128)}, f32[512,1280]{1,0:T(8,128)}, f32[512,1280]{1,0:T(8,128)})) %all-reduce.14.cloned.1.call-update) | async-done | bytes 7864336
  353.0 120.1 %scatter_custom_fusion = s32[2049]{0:T(1024)S(1)} fusion(s32[32768]{0:T(1024)S(1)} %bitcast.296, s32[32768]{0:T(1024)S(1)} %reshape.1134, s32[]{:T(128)} %constant.196.clone.1), kind=kCustom, calls=%fused_computation.206 | custom fusion | bytes 8200 | tf_op jit(solution)/shard_map/scatter | solution.py:57
  475.0 1.9 gather_fusion.15
  477.0 1.9 gather_fusion.7
  478.9 1.9 gather_fusion.1
  482.0 120.1 %scatter_custom_fusion.1 = s32[2049]{0:T(1024)S(1)} fusion(s32[32768]{0:T(1024)S(1)} %bitcast.297, s32[32768]{0:T(1024)S(1)} %reshape.1142, s32[]{:T(128)} %constant.197.clone.1), kind=kCustom, calls=%fused_computation.204 | custom fusion | bytes 8200 | tf_op jit(solution)/shard_map/scatter | solution.py:58
  615.2 1.9 fusion.9
  619.3 2.3 reshape.931
  621.6 2.8 gather_fusion.4
  624.4 2.8 fusion.6
  629.4 49.9 %all-gather.15.cloned.1.call-done = bf16[512,1024]{1,0:T(8,128)(2,1)} async-done(((bf16[8,1024]{1,0:T(8,128)(2,1)}), bf16[512,1024]{1,0:T(8,128)(2,1)}) %all-gather.15.cloned.1.call-update) | async-done | bytes 1048592 | tf_op jit(solution)/shard_map/all_gather | solution.py:108
  679.3 2.3 reshape.950
  681.6 2.8 gather_fusion.17
  684.4 2.9 fusion.12
  689.4 2.5 select_reduce_fusion.2
  697.5 1.6 copy.304
  705.7 1.6 copy.319
  707.4 1.7 reshape.952
  715.8 244.4 %all-reduce.9 = (f32[512,8]{0,1:T(8,128)}, f32[512,8]{0,1:T(8,128)}, f32[512,8]{0,1:T(8,128)}) all-reduce(f32[512,8]{0,1:T(8,128)} %dynamic_update_slice.11, f32[512,8]{0,1:T(8,128)S(1)} %dynamic_update_slice.10, f32[512,8]{0,1:T(8,128)} %copy-done.7), channel_id=1, replica_groups=mesh['kv'=4,'blk'=64] {'blk'}, use_global_device_ids=true, to_apply=%region_30.31 | all-reduce | flops 12288 | bytes 98304 | tf_op jit(solution)/shard_map/pmax | solution.py:136
  961.9 2.3 gather_fusion.5
  964.2 1.8 fusion.28
  966.0 3.1 fusion.21
  969.0 2.7 reshape.936
  973.4 2.3 gather_fusion.12
  977.2 3.1 fusion.18
  980.3 2.7 reshape.945
  984.6 2.3 gather_fusion.19
  986.9 1.7 fusion.24
  988.6 1.7 fusion.15
  1006.3 252.8 %all-reduce.6 = (f32[512,8]{1,0:T(8,128)S(1)}, f32[512,8]{1,0:T(8,128)S(1)}, f32[512,8]{1,0:T(8,128)S(1)}) all-reduce(f32[512,8]{1,0:T(8,128)S(1)} %reshape.957, f32[512,8]{1,0:T(8,128)S(1)} %reshape.947, f32[512,8]{1,0:T(8,128)S(1)} %reshape.937), channel_id=10, replica_groups=mesh['kv'=4,'blk'=64] {'blk'}, use_global_device_ids=true, to_apply=%region_33.34.clone | all-reduce | flops 12288 | bytes 98304
  1268.0 133.9 %reduce-scatter.8.cloned.1.call-done = f32[8,8,128]{2,1,0:T(8,128)} async-done(((f32[512,8,128]{2,1,0:T(8,128)}), f32[8,8,128]{2,1,0:T(8,128)}) %reduce-scatter.8.cloned.1.call-update) | async-done | bytes 32784 | tf_op jit(solution)/shard_map/reduce_scatter | solution.py:168
  1403.6 76.2 %all-gather.9.cloned.1.call-done = bf16[512,1024]{1,0:T(8,128)(2,1)} async-done(((bf16[8,1024]{1,0:T(8,128)(2,1)}), bf16[512,1024]{1,0:T(8,128)(2,1)}) %all-gather.9.cloned.1.call-update) | async-done | bytes 1048592 | tf_op jit(solution)/shard_map/all_gather | solution.py:176
  1479.8 2.3 fusion.158
  1482.1 74.9 %all-gather.13.cloned.1.call-done = bf16[512,1024]{1,0:T(8,128)(2,1)} async-done(((bf16[8,1024]{1,0:T(8,128)(2,1)}), bf16[512,1024]{1,0:T(8,128)(2,1)}) %all-gather.13.cloned.1.call-update) | async-done | bytes 1048592 | tf_op jit(solution)/shard_map/all_gather | solution.py:176
  1557.0 2.3 fusion.159
  1559.3 75.3 %all-gather.17.cloned.1.call-done = bf16[512,1024]{1,0:T(8,128)(2,1)} async-done(((bf16[8,1024]{1,0:T(8,128)(2,1)}), bf16[512,1024]{1,0:T(8,128)(2,1)}) %all-gather.17.cloned.1.call-update) | async-done | bytes 1048592 | tf_op jit(solution)/shard_map/all_gather | solution.py:176
  1634.7 2.3 fusion.160
  1637.7 46.4 %all-reduce.16.cloned.1.call-done = (f32[512,64]{0,1:T(8,128)}, f32[512,64]{0,1:T(8,128)}, f32[512,64]{0,1:T(8,128)}) async-done(((f32[512,64]{0,1:T(8,128)}, f32[512,64]{0,1:T(8,128)}, f32[512,64]{0,1:T(8,128)}), (f32[512,64]{0,1:T(8,128)}, f32[512,64]{0,1:T(8,128)}, f32[512,64]{0,1:T(8,128)})) %all-reduce.16.cloned.1.call-update) | async-done | bytes 393232 | tf_op jit(solution)/shard_map/psum | solution.py:178
  (255 shorter events, 84.6 us)
Async XLA Ops:
  7.2 1472.6 %copy-start = (bf16[1024,64]{0,1:T(8,128)(2,1)S(1)}, bf16[1024,64]{0,1:T(8,128)(2,1)}, u32[]{:S(2)}) copy-start(bf16[1024,64]{0,1:T(8,128)(2,1)} %param.27) | copy-start | bytes 393220
  7.2 135.0 %copy-start.5 = (bf16[3,512,64]{1,2,0:T(8,128)(2,1)S(1)}, bf16[3,512,64]{1,2,0:T(8,128)(2,1)}, u32[]{:S(2)}) copy-start(bf16[3,512,64]{1,2,0:T(8,128)(2,1)} %param.22) | copy-start | bytes 589828
  7.2 135.0 %copy-start.32 = (f32[64]{0:T(128)S(1)}, f32[64]{0:T(128)}, u32[]{:S(2)}) copy-start(f32[64]{0:T(128)} %param.23) | copy-start | bytes 772
  7.2 343.0 %all-reduce.14.cloned.1.call-start = ((), (), s32[]{:S(2)}) async-start(), calls=%async_computation.12 | async-start | bytes 15728640
  146.5 0.7 copy-start.15
  146.5 465.7 %all-gather.11.cloned.1.call-start = ((), (), s32[]{:S(2)}) async-start(), calls=%async_computation.6 | async-start | bytes 1064960 | tf_op jit(solution)/shard_map/all_gather | solution.py:108
  147.2 7.1 copy-start.1
  154.3 454.4 %copy-start.30 = (s32[1024]{0:T(1024)}, s32[1024]{0:T(1024)S(1)}, u32[]{:S(2)}) copy-start(s32[1024]{0:T(1024)S(1)} %get-tuple-element.185) | copy-start | bytes 12292
  161.4 7.0 copy-start.6
  161.4 7.4 copy-start.33
  352.7 266.6 %all-gather.7.cloned.1.call-start = ((), (), s32[]{:S(2)}) async-start(), calls=%async_computation.3 | async-start | bytes 1064960 | tf_op jit(solution)/shard_map/all_gather | solution.py:108
  473.2 129.1 %copy-start.17 = (pred[32]{0:T(512)(128)(4,1)}, pred[32]{0:T(512)(128)(4,1)S(1)}, u32[]{:S(2)}) copy-start(pred[32]{0:T(512)(128)(4,1)S(1)} %get-tuple-element.121) | copy-start | bytes 100
  473.2 129.1 %copy-start.22 = (s32[32]{0:T(128)}, s32[32]{0:T(128)S(1)}, u32[]{:S(2)}) copy-start(s32[32]{0:T(128)S(1)} %get-tuple-element.124) | copy-start | bytes 388
  474.8 204.5 %all-gather.15.cloned.1.call-start = ((), (), s32[]{:S(2)}) async-start(), calls=%async_computation.9 | async-start | bytes 1064960 | tf_op jit(solution)/shard_map/all_gather | solution.py:108
  482.0 133.2 %copy-start.2 = (bf16[32,1,2,128,128]{4,3,2,1,0:T(8,128)(2,1)S(1)}, bf16[32,1,2,128,128]{4,3,2,1,0:T(8,128)(2,1)}, u32[]{:S(2)}) copy-start(bf16[32,1,2,128,128]{4,3,2,1,0:T(8,128)(2,1)} %param.28) | copy-start | bytes 6291460
  602.3 9.9 copy-start.31
  604.8 655.3 %reduce-scatter.4.cloned.1.call-start = ((), (), s32[]{:S(2)}) async-start(), calls=%async_computation.4 | async-start | bytes 2129920 | tf_op jit(solution)/shard_map/reduce_scatter | solution.py:168
  604.8 10.4 copy-start.27
  609.4 2.8 copy-start.9
  696.9 0.6 copy-start.7
  960.3 5.7 copy-start.18
  960.3 5.7 copy-start.23
  971.8 0.7 copy-start.13
  971.8 292.3 %reduce-scatter.6.cloned.1.call-start = ((), (), s32[]{:S(2)}) async-start(), calls=%async_computation.7 | async-start | bytes 2129920 | tf_op jit(solution)/shard_map/reduce_scatter | solution.py:168
  973.4 3.8 copy-start.19
  973.4 3.8 copy-start.24
  983.0 0.7 copy-start.12
  983.0 419.0 %reduce-scatter.8.cloned.1.call-start = ((), (), s32[]{:S(2)}) async-start(), calls=%async_computation.10 | async-start | bytes 2129920 | tf_op jit(solution)/shard_map/reduce_scatter | solution.py:168
  984.6 4.0 copy-start.20
  984.6 4.0 copy-start.25
  991.9 7.2 copy-start.4
  991.9 13.3 copy-start.3
  991.9 487.9 %all-gather.9.cloned.1.call-start = ((), (), s32[]{:S(2)}) async-start(), calls=%async_computation.5 | async-start | bytes 1064960 | tf_op jit(solution)/shard_map/all_gather | solution.py:176
  1000.5 5.3 copy-start.21
  1000.5 5.3 copy-start.26
  1001.5 257.6 %copy-start.11 = (f32[8,1,8]{0,2,1:T(8,128)S(1)}, f32[8,1,8]{0,2,1:T(8,128)}, u32[]{:S(2)}) copy-start(f32[8,1,8]{0,2,1:T(8,128)} %copy.332) | copy-start | bytes 772
  1001.6 258.5 %copy-start.16 = (f32[8,128]{1,0:T(8,128)S(1)}, f32[8,128]{1,0:T(8,128)}, u32[]{:S(2)}) copy-start(f32[8,128]{1,0:T(8,128)} %get-tuple-element.131) | copy-start | bytes 12292
  1001.7 259.9 %copy-start.29 = (bf16[1,8,128]{2,1,0:T(8,128)(2,1)S(1)}, bf16[1,8,128]{2,1,0:T(8,128)(2,1)}, u32[]{:S(2)}) copy-start(bf16[1,8,128]{2,1,0:T(8,128)(2,1)} %get-tuple-element.132) | copy-start | bytes 6148
  1001.7 259.9 %copy-start.14 = (bf16[3,8,128]{2,0,1:T(4,128)(2,1)S(1)}, bf16[3,8,128]{2,0,1:T(4,128)(2,1)}, u32[]{:S(2)}) copy-start(bf16[3,8,128]{2,0,1:T(4,128)(2,1)} %copy.390) | copy-start | bytes 18436
  1001.7 262.3 %copy-start.28 = (f32[8,8,2]{1,2,0:T(2,128)S(1)}, f32[8,8,2]{1,2,0:T(2,128)}, u32[]{:S(2)}) copy-start(f32[8,8,2]{1,2,0:T(2,128)} %get-tuple-element.180) | copy-start | bytes 1540
  1002.6 265.4 %copy-start.8 = (f32[8,8,3]{1,2,0:T(4,128)S(1)}, f32[8,8,3]{1,2,0:T(4,128)}, u32[]{:S(2)}) copy-start(f32[8,8,3]{1,2,0:T(4,128)} %get-tuple-element.178) | copy-start | bytes 2308
  1261.5 295.5 %all-gather.13.cloned.1.call-start = ((), (), s32[]{:S(2)}) async-start(), calls=%async_computation.8 | async-start | bytes 1064960 | tf_op jit(solution)/shard_map/all_gather | solution.py:176
  1265.7 369.0 %all-gather.17.cloned.1.call-start = ((), (), s32[]{:S(2)}) async-start(), calls=%async_computation.11 | async-start | bytes 1064960 | tf_op jit(solution)/shard_map/all_gather | solution.py:176
  1403.5 233.5 %copy-start.10 = (bf16[3,8,128]{2,0,1:T(4,128)(2,1)S(1)}, bf16[3,8,128]{2,0,1:T(4,128)(2,1)}, u32[]{:S(2)}) copy-start(bf16[3,8,128]{2,0,1:T(4,128)(2,1)} %copy-done.9) | copy-start | bytes 18436
  1403.6 280.5 %all-reduce.16.cloned.1.call-start = ((), (), s32[]{:S(2)}) async-start(), calls=%async_computation.13 | async-start | bytes 786432 | tf_op jit(solution)/shard_map/psum | solution.py:178
Sparse Core Ops, SparseCore 0:
  146.6 203.5 all-reduce.13
  353.5 74.3 all-gather.10
  474.9 74.3 all-gather.6
  604.9 74.3 all-gather.14
  971.9 143.4 reduce-scatter.3
  1119.9 138.9 reduce-scatter.5
  1262.9 138.9 reduce-scatter.7
  1405.1 74.6 all-gather.8
  1482.9 74.0 all-gather.12
  1560.6 74.0 all-gather.16
  1637.9 46.1 all-reduce.15
where the time goes:
time: 1700 us; the launch traced here: 1690 us
  waiting for transfers between devices  637 us (37%)
  blocking collectives  626 us (37%)
  local copies, waits for them, and re-layouts  352 us (21%)
  matrix products  41.8 us (2%)
  other arithmetic  20.1 us (1%)
    unnamed x1, blocking collectives  253 us
    pmax x1, blocking collectives, body(): ceiling = lax.pmax(local_top, 'blk')  244 us
    all_gather x3, waiting for transfers between devices, body(): attended = lax.all_gather(own_rows, 'blk', axis=0, tiled=True)  226 us
    unnamed x12, waiting for transfers between devices  180 us
    reduce_scatter x3, waiting for transfers between devices, body(): lax.psum_scatter(numerator, 'blk', scatter_dimension=0, tiled=True)  134 us
    psum x1, blocking collectives, body(): squares = lax.psum(jnp.sum(stream * stream, axis=1), 'blk')  128 us
    scatter x1, local copies, waits for them, and re-layouts, body(): jnp.zeros((total_slots + 1,), jnp.int32).at[flat_table]  120 us
    scatter x1, local copies, waits for them, and re-layouts, body(): jnp.full((total_slots + 1,), -1, jnp.int32).at[flat_table]  120 us
  transfers between devices with their start and end apart: 11, of which 7 were waited for; matrix products, arithmetic and copies ran while one was open for 20% of the time, Pallas kernels for 0%

commit v1 on v0

--- a/solution.py
+++ b/solution.py
@@ -173,7 +173,15 @@
             .astype(jnp.bfloat16)
             .reshape(beams_here, heads_per_group * head_dim)
         )
-        attended = lax.all_gather(own_rows, "blk", axis=0, tiled=True)
+        attended = jnp.concatenate(
+            lax.all_to_all(
+                jnp.stack(lax.psum(1, axis_name="blk") * [own_rows], 0),
+                axis_name="blk",
+                split_axis=0,
+                concat_axis=0,
+            ),
+            axis=0,
+        )
         partial_value = jnp.dot(attended, w_out, preferred_element_type=jnp.float32)
         head_total = lax.psum(partial_value, "kv")
         outputs.append((stream + head_total).astype(jnp.bfloat16))

time: 1700 us -> 1520 us (0.89)
  waiting for transfers between devices: 637 us -> 429 us
  starting transfers between devices: 0.68 us -> 28 us
    all_gather x3 -> x0, waiting for transfers between devices: 226 us -> none  [body(): attended = lax.all_gather(own_rows, 'blk', axis=0, tiled=True)]
    all_to_all x0 -> x3, waiting for transfers between devices: none -> 44.4 us  [body(): lax.all_to_all(jnp.stack(lax.psum(1, axis_name='blk') * [own_rows], 0), a...]
    all_to_all x0 -> x3, starting transfers between devices: none -> 27.5 us  [body(): lax.all_to_all(jnp.stack(lax.psum(1, axis_name='blk') * [own_rows], 0), a...]
    reduce_scatter x3, waiting for transfers between devices: 134 us -> 107 us  [body(): lax.psum_scatter(numerator, 'blk', scatter_dimension=0, tiled=True)]
    unnamed x12 -> x9, waiting for transfers between devices: 180 us -> 180 us
  transfers between devices with their start and end apart: 11 -> 11, of which waited for: 7 -> 6; matrix products, arithmetic and copies ran while one was open for 20% -> 23% of each run, Pallas kernels for 0% -> 0%
where the time goes in v1:
time: 1520 us; the launch traced here: 1510 us
  blocking collectives  626 us (41%)
  waiting for transfers between devices  429 us (28%)
  local copies, waits for them, and re-layouts  349 us (23%)
  matrix products  40.5 us (3%)
  starting transfers between devices  28 us (2%)
  other arithmetic  23 us (2%)
  between operations  15.6 us (1%)
    unnamed x1, blocking collectives  254 us
    pmax x1, blocking collectives, body(): ceiling = lax.pmax(local_top, 'blk')  244 us
    unnamed x9, waiting for transfers between devices  180 us
    psum x1, blocking collectives, body(): squares = lax.psum(jnp.sum(stream * stream, axis=1), 'blk')  128 us
    scatter x1, local copies, waits for them, and re-layouts, body(): jnp.full((total_slots + 1,), -1, jnp.int32).at[flat_table]  120 us
    scatter x1, local copies, waits for them, and re-layouts, body(): jnp.zeros((total_slots + 1,), jnp.int32).at[flat_table]  120 us
    reduce_scatter x3, waiting for transfers between devices, body(): lax.psum_scatter(numerator, 'blk', scatter_dimension=0, tiled=True)  107 us
    all_gather x3, waiting for transfers between devices, body(): lax.all_gather(rotated_query.reshape(beams_here, heads_per_group * head_d...  53.8 us
  transfers between devices with their start and end apart: 11, of which 6 were waited for; matrix products, arithmetic and copies ran while one was open for 23% of the time, Pallas kernels for 0%

profile of v1, /device:TPU:2, one launch (start us, length us, event | category | flops | bytes accessed | tf_op | source)
XLA Modules:
  0.0 1512.0 jit_solution(1880767185828595789)
XLA Ops:
  9.2 128.5 %all-reduce.7 = (f32[512]{0:T(512)S(1)}, f32[512]{0:T(512)S(1)}, f32[512]{0:T(512)S(1)}) all-reduce(f32[512]{0:T(512)S(1)} %get-tuple-element.102, f32[512]{0:T(512)S(1)} %get-tuple-element.101, f32[512]{0:T(512)S(1)} %get-tuple-element.100), channel_id=1, replica_groups=mesh['kv'=4,'blk'=64] {'blk'}, use_global_device_ids=true, to_apply=%region_25.26 | all-reduce | flops 1536 | bytes 12288 | tf_op jit(solution)/shard_map/psum | solution.py:84
  139.2 3.0 fusion.79
  142.2 2.0 fusion.82
  144.2 2.2 fusion.85
  147.1 3.5 gather_fusion
  150.6 3.5 gather_fusion.6
  154.3 3.5 gather_fusion.3
  157.8 3.5 gather_fusion.14
  161.3 3.5 gather_fusion.16
  164.9 3.5 gather_fusion.8
  170.2 180.0 %all-reduce.14.cloned.1.call-done = (f32[512,1280]{1,0:T(8,128)}, f32[512,1280]{1,0:T(8,128)}, f32[512,1280]{1,0:T(8,128)}) async-done(((f32[512,1280]{1,0:T(8,128)}, f32[512,1280]{1,0:T(8,128)}, f32[512,1280]{1,0:T(8,128)}), (f32[512,1280]{1,0:T(8,128)}, f32[512,1280]{1,0:T(8,128)}, f32[512,1280]{1,0:T(8,128)})) %all-reduce.14.cloned.1.call-update) | async-done | bytes 7864336
  353.0 120.1 %scatter_custom_fusion = s32[2049]{0:T(1024)S(1)} fusion(s32[32768]{0:T(1024)S(1)} %bitcast.302, s32[32768]{0:T(1024)S(1)} %reshape.1140, s32[]{:T(128)} %constant.196.clone.1), kind=kCustom, calls=%fused_computation.212 | custom fusion | bytes 8200 | tf_op jit(solution)/shard_map/scatter | solution.py:57
  475.0 1.9 gather_fusion.15
  477.0 1.9 gather_fusion.7
  478.9 1.9 gather_fusion.1
  482.0 120.1 %scatter_custom_fusion.1 = s32[2049]{0:T(1024)S(1)} fusion(s32[32768]{0:T(1024)S(1)} %bitcast.303, s32[32768]{0:T(1024)S(1)} %reshape.1148, s32[]{:T(128)} %constant.197.clone.1), kind=kCustom, calls=%fused_computation.210 | custom fusion | bytes 8200 | tf_op jit(solution)/shard_map/scatter | solution.py:58
  615.1 2.8 fusion.9
  621.8 2.9 fusion.6
  625.5 53.7 %all-gather.8.cloned.1.call-done = bf16[512,1024]{1,0:T(8,128)(2,1)} async-done(((bf16[8,1024]{1,0:T(8,128)(2,1)}), bf16[512,1024]{1,0:T(8,128)(2,1)}) %all-gather.8.cloned.1.call-update) | async-done | bytes 1048592 | tf_op jit(solution)/shard_map/all_gather | solution.py:108
  682.2 1.9 fusion.12
  686.4 2.5 select_reduce_fusion.2
  688.9 1.6 copy.294
  694.4 1.6 copy.304
  702.6 1.6 copy.319
  704.2 1.7 reshape.958
  712.7 244.4 %all-reduce.9 = (f32[512,8]{0,1:T(8,128)}, f32[512,8]{0,1:T(8,128)}, f32[512,8]{0,1:T(8,128)}) all-reduce(f32[512,8]{0,1:T(8,128)} %dynamic_update_slice.11, f32[512,8]{0,1:T(8,128)S(1)} %dynamic_update_slice.10, f32[512,8]{0,1:T(8,128)} %copy-done.5), channel_id=1, replica_groups=mesh['kv'=4,'blk'=64] {'blk'}, use_global_device_ids=true, to_apply=%region_30.31 | all-reduce | flops 12288 | bytes 98304 | tf_op jit(solution)/shard_map/pmax | solution.py:136
  958.7 2.3 gather_fusion.5
  961.0 1.8 fusion.28
  962.8 3.1 fusion.21
  965.8 2.7 reshape.942
  970.1 2.3 gather_fusion.12
  972.4 1.7 fusion.26
  974.1 3.0 fusion.18
  977.2 2.8 reshape.951
  981.3 1.6 copy.298
  985.4 1.9 fusion.8
  991.3 1.9 fusion.11
  996.5 2.3 gather_fusion.19
  1002.4 253.6 %all-reduce.6 = (f32[512,8]{1,0:T(8,128)}, f32[512,8]{1,0:T(8,128)}, f32[512,8]{1,0:T(8,128)}) all-reduce(f32[512,8]{1,0:T(8,128)} %reshape.963, f32[512,8]{1,0:T(8,128)} %reshape.953, f32[512,8]{1,0:T(8,128)} %reshape.943), channel_id=10, replica_groups=mesh['kv'=4,'blk'=64] {'blk'}, use_global_device_ids=true, to_apply=%region_33.34.clone | all-reduce | flops 12288 | bytes 98304
  1259.6 13.4 all-to-all-start
  1274.6 1.7 fusion.15
  1282.6 19.1 %all-to-all-done = bf16[64,8,1024]{2,1,0:T(8,128)(2,1)} async-done(((bf16[64,8,1024]{2,1,0:T(8,128)(2,1)}), bf16[64,8,1024]{2,1,0:T(8,128)(2,1)}, u32[]{:S(2)}, u32[]{:S(2)}) %all-to-all-start) | async-done | bytes 1048608 | tf_op jit(solution)/shard_map/all_to_all | solution.py:177
  1302.8 5.7 all-to-all-start.1
  1311.5 107.5 %reduce-scatter.8.cloned.1.call-done = f32[8,8,128]{2,1,0:T(8,128)} async-done(((f32[512,8,128]{2,1,0:T(8,128)}), f32[8,8,128]{2,1,0:T(8,128)}) %reduce-scatter.8.cloned.1.call-update) | async-done | bytes 32784 | tf_op jit(solution)/shard_map/reduce_scatter | solution.py:168
  1421.0 8.4 all-to-all-start.2
  1429.5 2.3 fusion.43
  1432.9 25.3 %all-to-all-done.2 = bf16[64,8,1024]{2,1,0:T(8,128)(2,1)S(1)} async-done(((bf16[64,8,1024]{2,1,0:T(8,128)(2,1)}), bf16[64,8,1024]{2,1,0:T(8,128)(2,1)S(1)}, u32[]{:S(2)}, u32[]{:S(2)}) %all-to-all-start.2) | async-done | bytes 1048608 | tf_op jit(solution)/shard_map/all_to_all | solution.py:177
  1460.0 43.4 %all-reduce.16.cloned.1.call-done = (f32[512,64]{0,1:T(8,128)}, f32[512,64]{0,1:T(8,128)}, f32[512,64]{0,1:T(8,128)}) async-done(((f32[512,64]{0,1:T(8,128)}, f32[512,64]{0,1:T(8,128)}, f32[512,64]{0,1:T(8,128)}), (f32[512,64]{0,1:T(8,128)}, f32[512,64]{0,1:T(8,128)}, f32[512,64]{0,1:T(8,128)})) %all-reduce.16.cloned.1.call-update) | async-done | bytes 393232 | tf_op jit(solution)/shard_map/psum | solution.py:186
  (243 shorter events, 91.2 us)
Async XLA Ops:
  7.2 1422.3 %copy-start = (bf16[1024,64]{0,1:T(8,128)(2,1)S(1)}, bf16[1024,64]{0,1:T(8,128)(2,1)}, u32[]{:S(2)}) copy-start(bf16[1024,64]{0,1:T(8,128)(2,1)} %param.27) | copy-start | bytes 393220
  7.2 135.0 %copy-start.3 = (bf16[3,512,64]{1,2,0:T(8,128)(2,1)S(1)}, bf16[3,512,64]{1,2,0:T(8,128)(2,1)}, u32[]{:S(2)}) copy-start(bf16[3,512,64]{1,2,0:T(8,128)(2,1)} %param.22) | copy-start | bytes 589828
  7.2 135.0 %copy-start.26 = (f32[64]{0:T(128)S(1)}, f32[64]{0:T(128)}, u32[]{:S(2)}) copy-start(f32[64]{0:T(128)} %param.23) | copy-start | bytes 772
  7.2 343.0 %all-reduce.14.cloned.1.call-start = ((), (), s32[]{:S(2)}) async-start(), calls=%async_computation.12 | async-start | bytes 15728640
  146.4 0.7 copy-start.12
  146.4 465.8 %all-gather.6.cloned.1.call-start = ((), (), s32[]{:S(2)}) async-start(), calls=%async_computation.8 | async-start | bytes 1064960 | tf_op jit(solution)/shard_map/all_gather | solution.py:108
  147.1 7.1 copy-start.1
  154.3 454.5 %copy-start.24 = (s32[1024]{0:T(1024)}, s32[1024]{0:T(1024)S(1)}, u32[]{:S(2)}) copy-start(s32[1024]{0:T(1024)S(1)} %get-tuple-element.185) | copy-start | bytes 12292
  161.3 7.0 copy-start.4
  161.3 7.4 copy-start.27
  352.7 266.1 %all-gather.4.cloned.1.call-start = ((), (), s32[]{:S(2)}) async-start(), calls=%async_computation.6 | async-start | bytes 1064960 | tf_op jit(solution)/shard_map/all_gather | solution.py:108
  473.2 129.1 %copy-start.13 = (pred[32]{0:T(512)(128)(4,1)}, pred[32]{0:T(512)(128)(4,1)S(1)}, u32[]{:S(2)}) copy-start(pred[32]{0:T(512)(128)(4,1)S(1)} %get-tuple-element.121) | copy-start | bytes 100
  473.2 129.1 %copy-start.17 = (s32[32]{0:T(128)}, s32[32]{0:T(128)S(1)}, u32[]{:S(2)}) copy-start(s32[32]{0:T(128)S(1)} %get-tuple-element.124) | copy-start | bytes 388
  474.8 204.5 %all-gather.8.cloned.1.call-start = ((), (), s32[]{:S(2)}) async-start(), calls=%async_computation.10 | async-start | bytes 1064960 | tf_op jit(solution)/shard_map/all_gather | solution.py:108
  482.0 133.2 %copy-start.2 = (bf16[32,1,2,128,128]{4,3,2,1,0:T(8,128)(2,1)S(1)}, bf16[32,1,2,128,128]{4,3,2,1,0:T(8,128)(2,1)}, u32[]{:S(2)}) copy-start(bf16[32,1,2,128,128]{4,3,2,1,0:T(8,128)(2,1)} %param.28) | copy-start | bytes 6291460
  602.3 9.9 copy-start.25
  604.7 652.9 %reduce-scatter.4.cloned.1.call-start = ((), (), s32[]{:S(2)}) async-start(), calls=%async_computation.7 | async-start | bytes 2129920 | tf_op jit(solution)/shard_map/reduce_scatter | solution.py:168
  604.8 76.0 %copy-start.21 = (s32[1024]{0:T(1024)}, s32[1024]{0:T(1024)S(1)}, u32[]{:S(2)}) copy-start(s32[1024]{0:T(1024)S(1)} %pad_clamp_fusion.7) | copy-start | bytes 12292
  609.4 2.8 copy-start.7
  693.8 0.6 copy-start.5
  957.1 5.6 copy-start.14
  957.1 5.6 copy-start.18
  968.5 0.7 copy-start.10
  968.6 313.1 %reduce-scatter.6.cloned.1.call-start = ((), (), s32[]{:S(2)}) async-start(), calls=%async_computation.9 | async-start | bytes 2129920 | tf_op jit(solution)/shard_map/reduce_scatter | solution.py:168
  970.1 4.0 copy-start.15
  970.1 4.0 copy-start.19
  999.9 256.8 %copy-start.9 = (f32[8,1,8]{0,2,1:T(8,128)S(1)}, f32[8,1,8]{0,2,1:T(8,128)}, u32[]{:S(2)}) copy-start(f32[8,1,8]{0,2,1:T(8,128)} %copy.332) | copy-start | bytes 772
  1259.6 42.1 %all-to-all-start = ((bf16[64,8,1024]{2,1,0:T(8,128)(2,1)}), bf16[64,8,1024]{2,1,0:T(8,128)(2,1)}, u32[]{:S(2)}, u32[]{:S(2)}) async-start(bf16[64,8,1024]{2,1,0:T(8,128)(2,1)} %stack.30), calls=%async_computation.1 | async-start | bytes 2097152 | tf_op jit(solution)/shard_map/all_to_all | solution.py:177
  1273.0 1.6 copy-start.16
  1273.0 1.6 copy-start.20
  1273.0 145.9 %reduce-scatter.8.cloned.1.call-start = ((), (), s32[]{:S(2)}) async-start(), calls=%async_computation.11 | async-start | bytes 2129920 | tf_op jit(solution)/shard_map/reduce_scatter | solution.py:168
  1277.9 0.7 copy-start.23
  1277.9 0.7 copy-start.11
  1277.9 3.1 copy-start.22
  1277.9 32.9 %copy-start.6 = (f32[8,8,3]{1,2,0:T(4,128)S(1)}, f32[8,8,3]{1,2,0:T(4,128)}, u32[]{:S(2)}) copy-start(f32[8,8,3]{1,2,0:T(4,128)} %get-tuple-element.178) | copy-start | bytes 2308
  1302.8 117.1 %all-to-all-start.1 = ((bf16[64,8,1024]{2,1,0:T(8,128)(2,1)}), bf16[64,8,1024]{2,1,0:T(8,128)(2,1)S(1)}, u32[]{:S(2)}, u32[]{:S(2)}) async-start(bf16[64,8,1024]{2,1,0:T(8,128)(2,1)} %stack.32), calls=%async_computation.3 | async-start | bytes 2097152 | tf_op jit(solution)/shard_map/all_to_all | solution.py:177
  1421.0 37.2 %all-to-all-start.2 = ((bf16[64,8,1024]{2,1,0:T(8,128)(2,1)}), bf16[64,8,1024]{2,1,0:T(8,128)(2,1)S(1)}, u32[]{:S(2)}, u32[]{:S(2)}) async-start(bf16[64,8,1024]{2,1,0:T(8,128)(2,1)} %stack.34), calls=%async_computation.5 | async-start | bytes 2097152 | tf_op jit(solution)/shard_map/all_to_all | solution.py:177
  1429.4 29.9 %copy-start.8 = (bf16[3,8,128]{2,0,1:T(4,128)(2,1)S(1)}, bf16[3,8,128]{2,0,1:T(4,128)(2,1)}, u32[]{:S(2)}) copy-start(bf16[3,8,128]{2,0,1:T(4,128)(2,1)} %copy-done.7) | copy-start | bytes 18436
  1429.5 74.0 %all-reduce.16.cloned.1.call-start = ((), (), s32[]{:S(2)}) async-start(), calls=%async_computation.13 | async-start | bytes 786432 | tf_op jit(solution)/shard_map/psum | solution.py:186
Sparse Core Ops, SparseCore 0:
  146.5 203.5 all-reduce.13
  352.9 74.3 all-gather.5
  474.9 74.3 all-gather.3
  604.9 74.3 all-gather.7
  968.7 143.5 reduce-scatter.3
  1116.8 138.9 reduce-scatter.5
  1278.0 140.8 reduce-scatter.7
  1459.5 43.8 all-reduce.15
